TPU v7x, 128 devices: a whole 4x4x4 slice. The times are simulated.
128 devices in a mesh: blk: 8 (over z, core), grp: 16 (over x, y).
Axes of the slice: x: 4, y: 4, z: 4, core: 2. Of those that a mesh axis runs over, the one named last changes fastest.
Arguments:
- user_prior: float32 [32768, 128], P(('blk', 'grp')), may hold values from -6 to 6
- item_factors: bfloat16 [524288, 128], P(('blk', 'grp')), may hold values from -0.375 to 0.375
- user_tiles: int32 [8192], P(('blk', 'grp')), may hold values from 0 to 31
- item_tiles: int32 [8192], P(('blk', 'grp')), may hold values from 0 to 4095, as said below
- counts: int32 [8192, 128, 128], P(('blk', 'grp')), may hold values from 0 to 20, as said below
Outputs:
- user_factors: float32 [32768, 128], P(('blk', 'grp'))
Inputs may be any that keep to these rules, and one draw needn't show every extreme that they name: `item_tiles`: item tile t is held by device t // 32 of blk+grp. The entries of one device name tiles of 32 different holders, exactly 2 entries for each holder that they name, in no particular order. In each device's 64 entries, those whose tile of counts has a nonzero value come before those whose tile is all zero; in every group along grp at least one device has all 64 entries of the first kind.
All inputs are finite; a program needn't handle non-finite values.
Results may differ from a plain program's by a relative error of at most 0.0003.
The roundings to bfloat16 on the way count: a program that leaves them out, or rounds other values in their place, can miss the bound.
Values may be sent and summed in bfloat16 or wider, within the bound.
A program may use at most 128 MiB of HBM per device.

v0:
```python
import jax
import jax.numpy as jnp
from jax import lax
from jax.sharding import PartitionSpec as P

ITERS = 3
ALPHA = 40.0
REG = 32.0
EPS = 1e-06


def fetch_tiles(item_factors, item_tiles, pairs, tile, rank):
    n_all = lax.axis_size(("blk", "grp"))
    tiles_held = item_factors.shape[0] // tile
    slots_each = max(2, pairs // n_all)
    owner = item_tiles // tiles_held
    local_slot = item_tiles % tiles_held
    position = jnp.arange(pairs, dtype=jnp.int32)
    earlier = (owner[None, :] == owner[:, None]) & (position[None, :] < position[:, None])
    order = jnp.sum(earlier.astype(jnp.int32), axis=1)
    requests = jnp.full((n_all, slots_each), -1, jnp.int32).at[owner, order].set(local_slot)
    wanted = lax.all_to_all(requests, ("blk", "grp"), split_axis=0, concat_axis=0, tiled=True)
    held = item_factors.reshape(tiles_held, tile, rank)
    picked = jnp.take(held, jnp.maximum(wanted, 0), axis=0)
    picked = jnp.where((wanted >= 0)[:, :, None, None], picked, jnp.zeros((), picked.dtype))
    arrived = lax.all_to_all(picked, ("blk", "grp"), split_axis=0, concat_axis=0, tiled=True)
    return arrived[owner, order]


def body(user_prior, item_factors, user_tiles, item_tiles, counts):
    pairs = counts.shape[0]
    tile = counts.shape[1]
    rank = item_factors.shape[1]
    n_grp = lax.axis_size("grp")
    own_rows = user_prior.shape[0]
    block_rows = own_rows * n_grp
    user_blocks = block_rows // tile
    span = min(32, pairs)
    gram_local = lax.dot_general(
        item_factors, item_factors, (((0,), (0,)), ((), ())), preferred_element_type=jnp.float32
    )
    gram = lax.psum(gram_local, ("blk", "grp"))
    pair_tiles = fetch_tiles(item_factors, item_tiles, pairs, tile, rank)
    live = jnp.sum(jnp.any(counts > 0, axis=(1, 2)).astype(jnp.int32))
    rounds = (live + span - 1) // span
    tile_ids = jnp.arange(user_blocks, dtype=jnp.int32)

    def accumulate(low_tiles, with_rhs):

        def one_round(index, totals):
            start = index * span
            users = lax.dynamic_slice_in_dim(user_tiles, start, span)
            factors = lax.dynamic_slice_in_dim(pair_tiles, start, span)
            counted = lax.dynamic_slice_in_dim(counts, start, span).astype(jnp.float32)
            selector = (tile_ids[:, None] == users[None, :]).astype(jnp.float32)
            users_low = jnp.take(low_tiles, users, axis=0)
            scores = jnp.einsum(
                "bur,bir->bui", users_low, factors, preferred_element_type=jnp.float32
            )
            scaled = (ALPHA * counted * scores).astype(jnp.bfloat16)
            back = jnp.einsum("bui,bir->bur", scaled, factors, preferred_element_type=jnp.float32)
            result = [
                totals[0]
                + jnp.einsum("tb,bur->tur", selector, back, precision=lax.Precision.HIGHEST)
            ]
            if with_rhs:
                confidence = jnp.where(counted > 0, 1.0 + ALPHA * counted, 0.0).astype(jnp.bfloat16)
                pulled = jnp.einsum(
                    "bui,bir->bur", confidence, factors, preferred_element_type=jnp.float32
                )
                result.append(
                    totals[1]
                    + jnp.einsum("tb,bur->tur", selector, pulled, precision=lax.Precision.HIGHEST)
                )
            return tuple(result)

        zeros = jnp.zeros((user_blocks, tile, rank), jnp.float32)
        start_state = (zeros, zeros) if with_rhs else (zeros,)
        totals = lax.fori_loop(0, rounds, one_round, start_state)
        return tuple((total.reshape(block_rows, rank) for total in totals))

    def gram_term(vectors):
        return jnp.dot(vectors, gram, precision=lax.Precision.HIGHEST) + REG * vectors

    def row_sum(left, right):
        return jnp.sum(left * right, axis=1, keepdims=True)

    whole = lax.all_gather(user_prior, "grp", axis=0, tiled=True)
    pair_part, rhs_part = accumulate(
        whole.astype(jnp.bfloat16).reshape(user_blocks, tile, rank), True
    )
    pair_total, rhs_total = lax.psum((pair_part, rhs_part), "grp")
    solution = whole
    residual = rhs_total - (gram_term(solution) + pair_total)
    direction = residual
    norm_now = row_sum(residual, residual)
    for step in range(ITERS):
        (pair_part,) = accumulate(
            direction.astype(jnp.bfloat16).reshape(user_blocks, tile, rank), False
        )
        image = gram_term(direction) + lax.psum(pair_part, "grp")
        alpha = norm_now / (row_sum(direction, image) + EPS)
        solution = solution + alpha * direction
        residual = residual - alpha * image
        fresh = row_sum(residual, residual)
        direction = residual + fresh / (norm_now + EPS) * direction
        norm_now = fresh
    return lax.dynamic_slice_in_dim(solution, lax.axis_index("grp") * own_rows, own_rows, 0)


def solution(mesh):
    in_specs = (
        P(("blk", "grp"), None),
        P(("blk", "grp"), None),
        P(("blk", "grp")),
        P(("blk", "grp")),
        P(("blk", "grp"), None, None),
    )
    out_specs = P(("blk", "grp"), None)
    return jax.shard_map(body, mesh=mesh, in_specs=in_specs, out_specs=out_specs, check_vma=False)
```

profile of v0, /device:TPU:0, one launch (start us, length us, event | category | flops | bytes accessed | tf_op | source)
XLA Modules:
  0.0 787.2 jit_solution(2010041510047153230)
XLA Ops:
  7.4 3.5 compare_reduce_fusion
  10.9 0.7 and_select_fusion
  11.8 3.5 scatter_fusion
  15.4 20.5 %all_to_all.14 = s32[128,1,2]{2,1,0:T(1,128)S(1)} all-to-all(s32[128,1,2]{2,1,0:T(1,128)S(1)} %copy.108), channel_id=1, replica_groups=mesh['blk'=8,'grp'=16] {'blk','grp'}, dimensions={0} | all-to-all | bytes 2048 | tf_op jit(solution)/shard_map/all_to_all | solution.py:22
  36.5 8.4 %gather_fusion.4 = bf16[256,128,128]{2,1,0:T(8,128)(2,1)} fusion(bf16[32,128,128]{2,1,0:T(8,128)(2,1)S(1)} %bitcast.108, s32[1024]{0:T(1024)S(1)} %pad_clamp_fusion.4), kind=kCustom, calls=%fused_computation.4 | custom fusion | bytes 16778240 | tf_op jit(solution)/shard_map/jit(_take)/gather | solution.py:24
  44.9 7.4 select_select_fusion
  52.3 6.1 all-to-all-start.1
  58.4 0.8 copy.107
  59.3 1.1 fusion.134
  61.1 104.8 %all-gather.2.cloned.1.call-done = f32[4096,128]{0,1:T(8,128)} async-done(((f32[256,128]{0,1:T(8,128)}), f32[4096,128]{0,1:T(8,128)}) %all-gather.2.cloned.1.call-update) | async-done | bytes 2097168 | tf_op jit(solution)/shard_map/all_gather | solution.py:88
  165.9 1.7 convert_element_type.50
  167.7 1.3 copy.128
  169.0 4.3 gather_fusion.5
  173.3 1.6 broadcast.131.clone
  175.0 1.6 broadcast.131.clone.1
  176.5 18.2 %while.46 = (s32[]{:T(128)}, f32[32,128,128]{2,0,1:T(8,128)}, f32[32,128,128]{2,0,1:T(8,128)}, s32[]{:T(128)}, s32[64]{0:T(128)S(1)}, /*index=5*/s32[64,128,128]...) while((s32[]{:T(128)}, f32[32,128,128]{2,0,1:T(8,128)}, ...), condition=%wide.region_5.7_spmd.clone, body=%wide.region_4.6_spmd.clone.sunk | while | flops 812125440 | bytes 44048128 | solution.py:79
  176.8 2.0 gather_fusion
  178.8 4.1 fusion.186
  182.9 6.1 fusion.187
  188.9 0.5 fusion.188
  189.4 5.4 fusion.189
  194.8 3.5 copy.116
  198.3 4.6 copy.165
  202.8 3.5 copy.115
  206.3 4.6 copy.166
  211.2 58.5 %all-reduce.7.cloned.1.call-done = f32[128,128]{1,0:T(8,128)} async-done(((f32[128,128]{1,0:T(8,128)}), f32[128,128]{1,0:T(8,128)}) %all-reduce.7.cloned.1.call-update) | async-done | bytes 65552 | tf_op jit(solution)/shard_map/psum | solution.py:42
  269.7 105.7 %all-reduce.15.cloned.1.call-done = (f32[4096,128]{0,1:T(8,128)}, f32[4096,128]{0,1:T(8,128)}) async-done(((f32[4096,128]{0,1:T(8,128)}, f32[4096,128]{0,1:T(8,128)}), (f32[4096,128]{0,1:T(8,128)}, f32[4096,128]{0,1:T(8,128)})) %all-reduce.15.cloned.1.call-update) | async-done | bytes 4194320 | tf_op jit(solution)/shard_map/psum | solution.py:92
  375.5 7.0 fusion.133
  382.5 1.3 copy.129
  383.8 1.6 broadcast.131.clone.2
  385.4 12.0 %while.47 = (s32[]{:T(128)}, f32[32,128,128]{2,0,1:T(8,128)}, s32[]{:T(128)}, s32[64]{0:T(128)S(1)}, s32[64,128,128]{2,1,0:T(8,128)}, /*index=5*/bf16[32,128,128...) while((s32[]{:T(128)}, f32[32,128,128]{2,0,1:T(8,128)}, ...), condition=%wide.region_11.13_spmd.clone, body=%wide.region_10.12_spmd.clone.sunk | while | flops 472910112 | bytes 15735391 | solution.py:79
  385.5 2.0 gather_fusion.1
  387.4 4.1 fusion.195
  391.5 5.9 fusion.196
  397.4 3.4 copy.119
  400.8 4.6 copy.164
  405.4 0.4 all-reduce.11.cloned.1.call-start
  405.9 102.4 %all-reduce.9.cloned.1.call-done = f32[4096,128]{0,1:T(8,128)} async-done(((f32[4096,128]{0,1:T(8,128)}), f32[4096,128]{0,1:T(8,128)}) %all-reduce.9.cloned.1.call-update) | async-done | bytes 2097168 | tf_op jit(solution)/shard_map/psum | solution.py:101
  508.3 5.5 multiply_reduce_fusion.3
  514.2 1.9 fusion.132
  516.2 1.3 copy.130
  517.5 1.6 broadcast.131.clone.3
  519.1 12.1 %while.48 = (s32[]{:T(128)}, f32[32,128,128]{2,0,1:T(8,128)}, s32[]{:T(128)}, s32[64]{0:T(128)S(1)}, s32[64,128,128]{2,1,0:T(8,128)}, /*index=5*/bf16[32,128,128...) while((s32[]{:T(128)}, f32[32,128,128]{2,0,1:T(8,128)}, ...), condition=%wide.region_16.18_spmd.clone, body=%wide.region_15.17_spmd.clone.sunk | while | flops 472910112 | bytes 15735391 | solution.py:79
  519.2 2.0 gather_fusion.2
  521.2 4.1 fusion.202
  525.3 5.9 fusion.203
  531.2 3.4 copy.122
  534.7 4.6 copy.163
  539.5 101.9 %all-reduce.11.cloned.1.call-done = f32[4096,128]{0,1:T(8,128)} async-done(((f32[4096,128]{0,1:T(8,128)}), f32[4096,128]{0,1:T(8,128)}) %all-reduce.11.cloned.1.call-update) | async-done | bytes 2097168 | tf_op jit(solution)/shard_map/psum | solution.py:101
  641.4 5.3 multiply_reduce_fusion.1
  647.1 1.2 copy-done.6
  648.3 1.8 fusion.131
  650.2 1.3 copy.131
  651.5 1.6 broadcast.131
  653.1 12.3 %while.49 = (s32[]{:T(128)}, f32[32,128,128]{2,0,1:T(8,128)}, s32[]{:T(128)}, s32[64]{0:T(128)S(1)}, s32[64,128,128]{2,1,0:T(8,128)}, /*index=5*/bf16[32,128,128...) while((s32[]{:T(128)}, f32[32,128,128]{2,0,1:T(8,128)}, ...), condition=%wide.region_21.23_spmd.clone, body=%wide.region_20.22_spmd.clone.sunk | while | flops 472910112 | bytes 15735391 | solution.py:79
  653.2 2.0 gather_fusion.3
  655.2 4.1 fusion.209
  659.3 5.9 fusion.210
  665.4 2.7 copy.124
  668.1 3.0 copy.162
  671.3 102.4 %all-reduce.13.cloned.1.call-done = f32[4096,128]{0,1:T(8,128)} async-done(((f32[4096,128]{0,1:T(8,128)}), f32[4096,128]{0,1:T(8,128)}) %all-reduce.13.cloned.1.call-update) | async-done | bytes 2097168 | tf_op jit(solution)/shard_map/psum | solution.py:101
  773.7 4.0 fusion.123
  777.8 1.1 fusion.124
  778.8 0.8 copy.125
  (69 shorter events, 3.2 us)
Async XLA Ops:
  7.4 29.1 %copy-start = (bf16[4096,128]{1,0:T(8,128)(2,1)S(1)}, bf16[4096,128]{1,0:T(8,128)(2,1)}, u32[]{:S(2)}) copy-start(bf16[4096,128]{1,0:T(8,128)(2,1)} %param.16) | copy-start | bytes 3145732
  7.4 3.5 copy-start.11
  52.3 6.1 copy-start.10
  52.3 116.7 %all-to-all-start.1 = ((bf16[128,2,128,128]{3,2,1,0:T(8,128)(2,1)}), bf16[128,2,128,128]{3,2,1,0:T(8,128)(2,1)}, u32[]{:S(2)}, u32[]{:S(2)}) async-start(bf16[128,2,128,128]{3,2,1,0:T(8,128)(2,1)} %select_select_fusion), calls=%async_computation.1 | async-start | bytes 16777216 | tf_op jit(solution)/shard_map/all_to_all | solution.py:26
  58.4 107.5 %all-gather.2.cloned.1.call-start = ((), (), s32[]{:S(2)}) async-start(), calls=%async_computation.2 | async-start | bytes 2228224 | tf_op jit(solution)/shard_map/all_gather | solution.py:88
  59.2 210.5 %all-reduce.7.cloned.1.call-start = ((), (), s32[]{:S(2)}) async-start(), calls=%async_computation.3 | async-start | bytes 131072 | tf_op jit(solution)/shard_map/psum | solution.py:42
  60.4 315.1 %all-reduce.15.cloned.1.call-start = ((), (), s32[]{:S(2)}) async-start(), calls=%async_computation.7 | async-start | bytes 8388608 | tf_op jit(solution)/shard_map/psum | solution.py:92
  173.3 3.2 copy-start.9
  182.9 6.1 copy-start.2
  210.9 297.3 %all-reduce.9.cloned.1.call-start = ((), (), s32[]{:S(2)}) async-start(), calls=%async_computation.4 | async-start | bytes 4194304 | tf_op jit(solution)/shard_map/psum | solution.py:101
  405.4 102.9 %copy-start.8 = (f32[128,128]{1,0:T(8,128)S(1)}, f32[128,128]{1,0:T(8,128)}, u32[]{:S(2)}) copy-start(f32[128,128]{1,0:T(8,128)} %all-reduce.7.cloned.1.call-done) | copy-start | bytes 196612
  405.4 236.0 %all-reduce.11.cloned.1.call-start = ((), (), s32[]{:S(2)}) async-start(), calls=%async_computation.5 | async-start | bytes 4194304 | tf_op jit(solution)/shard_map/psum | solution.py:101
  508.3 5.5 copy-start.3
  514.2 2.0 copy-start.4
  539.3 234.4 %all-reduce.13.cloned.1.call-start = ((), (), s32[]{:S(2)}) async-start(), calls=%async_computation.6 | async-start | bytes 4194304 | tf_op jit(solution)/shard_map/psum | solution.py:101
  641.4 5.4 copy-start.5
  646.7 1.6 copy-start.6
  671.1 102.6 %copy-start.7 = (f32[4096,128]{0,1:T(8,128)S(1)}, f32[4096,128]{0,1:T(8,128)}, u32[]{:S(2)}) copy-start(f32[4096,128]{0,1:T(8,128)} %get-tuple-element.504) | copy-start | bytes 6291460
  773.7 5.9 copy-start.1
Sparse Core Ops, SparseCore 0:
  61.3 104.5 all-gather.1
  405.5 102.6 all-reduce.8
  671.2 102.3 all-reduce.12
Sparse Core Ops, SparseCore 1:
  64.5 205.2 all-reduce.6
  273.0 102.4 all-reduce.14
  539.3 102.0 all-reduce.10
where the time goes:
time: 795 us; the launch traced here: 787 us
  waiting for transfers between devices  576 us (72%)
  local copies, waits for them, and re-layouts  78.9 us (10%)
  matrix products  69 us (9%)
  blocking collectives  20.5 us (3%)
  other arithmetic  19.5 us (2%)
  between operations  16 us (2%)
    psum x3, waiting for transfers between devices, body(): image = gram_term(direction) + lax.psum(pair_part, 'grp')  307 us
    psum x1, waiting for transfers between devices, body(): pair_total, rhs_total = lax.psum((pair_part, rhs_part), 'grp')  106 us
    all_gather x1, waiting for transfers between devices, body(): whole = lax.all_gather(user_prior, 'grp', axis=0, tiled=True)  105 us
    psum x1, waiting for transfers between devices, body(): gram = lax.psum(gram_local, ('blk', 'grp'))  58.5 us
    unnamed x32, local copies, waits for them, and re-layouts  28.6 us
    dot_general x4, matrix products, one_round(): jnp.einsum('tb,bur->tur', selector, back, precision=lax.Precision.HIGHEST)  23.8 us
    dot_general x4, matrix products, gram_term(): jnp.dot(vectors, gram, precision=lax.Precision.HIGHEST) + REG * vectors  21.8 us
    all_to_all x1, blocking collectives, fetch_tiles(): lax.all_to_all(requests, ('blk', 'grp'), split_axis=0, concat_axis=0, til...  20.5 us
  transfers between devices with their start and end apart: 7, of which 6 were waited for; matrix products, arithmetic and copies ran while one was open for 6% of the time, Pallas kernels for 0%

commit v1 on v0

--- a/solution.py
+++ b/solution.py
@@ -39,7 +39,7 @@
     gram_local = lax.dot_general(
         item_factors, item_factors, (((0,), (0,)), ((), ())), preferred_element_type=jnp.float32
     )
-    gram = lax.psum(gram_local, ("blk", "grp"))
+    gram = jnp.sum(lax.all_gather(gram_local, axis_name=("blk", "grp")), 0)
     pair_tiles = fetch_tiles(item_factors, item_tiles, pairs, tile, rank)
     live = jnp.sum(jnp.any(counts > 0, axis=(1, 2)).astype(jnp.int32))
     rounds = (live + span - 1) // span

time: 795 us -> 746 us (0.938)
  waiting for transfers between devices: 576 us -> 532 us
  blocking collectives: 20.5 us -> 0 us
  starting transfers between devices: 7.1 us -> 18.1 us
    all_gather x1, waiting for transfers between devices: 105 us -> 0.02 us  [body(): whole = lax.all_gather(user_prior, 'grp', axis=0, tiled=True)]
    all_to_all x1, waiting for transfers between devices: 0.01 us -> 96.6 us  [fetch_tiles(): lax.all_to_all(picked, ('blk', 'grp'), split_axis=0, concat_axis=0, tiled...]
    psum x1 -> x0, waiting for transfers between devices: 58.5 us -> none  [body(): gram = lax.psum(gram_local, ('blk', 'grp'))]
    all_to_all x1 -> x0, blocking collectives: 20.5 us -> none  [fetch_tiles(): lax.all_to_all(requests, ('blk', 'grp'), split_axis=0, concat_axis=0, til...]
    psum x1, waiting for transfers between devices: 106 us -> 119 us  [body(): pair_total, rhs_total = lax.psum((pair_part, rhs_part), 'grp')]
    all_to_all x0 -> x1, starting transfers between devices: none -> 11.2 us  [fetch_tiles(): lax.all_to_all(requests, ('blk', 'grp'), split_axis=0, concat_axis=0, til...]
    all_to_all x0 -> x1, waiting for transfers between devices: none -> 8.33 us  [fetch_tiles(): lax.all_to_all(requests, ('blk', 'grp'), split_axis=0, concat_axis=0, til...]
    unnamed x32 -> x26, local copies, waits for them, and re-layouts: 28.6 us -> 29.7 us
  transfers between devices with their start and end apart: 7 -> 8, of which waited for: 6 -> 6; matrix products, arithmetic and copies ran while one was open for 6% -> 10% of each run, Pallas kernels for 0% -> 0%
where the time goes in v1:
time: 746 us; the launch traced here: 739 us
  waiting for transfers between devices  532 us (71%)
  local copies, waits for them, and re-layouts  80.5 us (11%)
  matrix products  70.4 us (9%)
  other arithmetic  23.2 us (3%)
  starting transfers between devices  18.1 us (2%)
  between operations  14.5 us (2%)
    psum x3, waiting for transfers between devices, body(): image = gram_term(direction) + lax.psum(pair_part, 'grp')  307 us
    psum x1, waiting for transfers between devices, body(): pair_total, rhs_total = lax.psum((pair_part, rhs_part), 'grp')  119 us
    all_to_all x1, waiting for transfers between devices, fetch_tiles(): lax.all_to_all(picked, ('blk', 'grp'), split_axis=0, concat_axis=0, tiled...  96.6 us
    unnamed x26, local copies, waits for them, and re-layouts  29.7 us
    dot_general x4, matrix products, one_round(): jnp.einsum('tb,bur->tur', selector, back, precision=lax.Precision.HIGHEST)  23.8 us
    dot_general x4, matrix products, gram_term(): jnp.dot(vectors, gram, precision=lax.Precision.HIGHEST) + REG * vectors  23 us
    dot_general x4, matrix products, one_round(): jnp.einsum('bui,bir->bur', scaled, factors, preferred_element_type=jnp.fl...  16.4 us
    while x5, local copies, waits for them, and re-layouts, accumulate(): totals = lax.fori_loop(0, rounds, one_round, start_state)  16.4 us
  transfers between devices with their start and end apart: 8, of which 6 were waited for; matrix products, arithmetic and copies ran while one was open for 10% of the time, Pallas kernels for 0%

profile of v1, /device:TPU:0, one launch (start us, length us, event | category | flops | bytes accessed | tf_op | source)
XLA Modules:
  0.0 738.7 jit_solution(9707504253034539134)
XLA Ops:
  6.5 1.7 copy.107
  8.3 3.4 compare_reduce_fusion
  11.8 0.6 and_select_fusion
  12.6 3.5 scatter_fusion
  16.1 0.7 copy.108
  16.8 11.2 %all-to-all-start = ((s32[128,1,2]{2,1,0:T(1,128)}), s32[128,1,2]{2,1,0:T(1,128)S(1)}, u32[]{:S(2)}, u32[]{:S(2)}) async-start(s32[128,1,2]{2,1,0:T(1,128)} %copy.108), calls=%async_computation | async-start | bytes 131072 | tf_op jit(solution)/shard_map/all_to_all | solution.py:22
  28.0 1.1 fusion.134
  29.2 8.3 %all-to-all-done = s32[128,1,2]{2,1,0:T(1,128)S(1)} async-done(((s32[128,1,2]{2,1,0:T(1,128)}), s32[128,1,2]{2,1,0:T(1,128)S(1)}, u32[]{:S(2)}, u32[]{:S(2)}) %all-to-all-start) | async-done | bytes 1056 | tf_op jit(solution)/shard_map/all_to_all | solution.py:22
  38.1 8.4 %gather_fusion.4 = bf16[256,128,128]{2,1,0:T(8,128)(2,1)} fusion(bf16[32,128,128]{2,1,0:T(8,128)(2,1)S(1)} %bitcast.109, s32[1024]{0:T(1024)S(1)} %pad_clamp_fusion.4), kind=kCustom, calls=%fused_computation.4 | custom fusion | bytes 16778240 | tf_op jit(solution)/shard_map/jit(_take)/gather | solution.py:24
  46.5 7.4 %select_select_fusion = bf16[128,2,128,128]{3,2,1,0:T(8,128)(2,1)} fusion(bf16[128,2,128,128]{3,2,1,0:T(8,128)(2,1)} %bitcast.115, pred[128,2]{1,0:T(8,128)(4,1)S(1)} %copy.112, pred[128,2]{1,0:T(8,128)(4,1)S(1)} %copy.110), kind=kLoop, calls=%fused_computation.103 | loop fusion | flops 8388608 | bytes 16777728 | tf_op jit(solution)/shard_map/jit(_where)/select_n | solution.py:25
  53.9 5.9 all-to-all-start.1
  60.6 1.7 convert_element_type.50
  62.3 1.3 copy.128
  63.6 96.6 %all-to-all-done.1 = bf16[128,2,128,128]{3,2,1,0:T(8,128)(2,1)} async-done(((bf16[128,2,128,128]{3,2,1,0:T(8,128)(2,1)}), bf16[128,2,128,128]{3,2,1,0:T(8,128)(2,1)}, u32[]{:S(2)}, u32[]{:S(2)}) %all-to-all-start.1) | async-done | bytes 8388640 | tf_op jit(solution)/shard_map/all_to_all | solution.py:26
  160.2 4.3 gather_fusion.5
  164.6 1.6 broadcast.131.clone
  166.2 1.6 broadcast.131.clone.1
  167.8 18.5 %while.46 = (s32[]{:T(128)}, f32[32,128,128]{2,0,1:T(8,128)}, f32[32,128,128]{2,0,1:T(8,128)}, s32[]{:T(128)}, s32[64]{0:T(128)S(1)}, /*index=5*/s32[64,128,128]...) while((s32[]{:T(128)}, f32[32,128,128]{2,0,1:T(8,128)}, ...), condition=%wide.region_5.7_spmd.clone, body=%wide.region_4.6_spmd.clone.sunk | while | flops 812125440 | bytes 44048128 | solution.py:79
  168.1 2.0 gather_fusion
  170.1 4.1 fusion.186
  174.2 6.1 fusion.187
  180.7 5.6 fusion.189
  186.3 3.5 copy.116
  189.7 4.7 copy.165
  194.4 3.4 copy.115
  197.8 4.5 copy.166
  202.7 3.8 reduce_sum.86
  206.5 119.0 %all-reduce.12.cloned.1.call-done = (f32[4096,128]{0,1:T(8,128)}, f32[4096,128]{0,1:T(8,128)}) async-done(((f32[4096,128]{0,1:T(8,128)}, f32[4096,128]{0,1:T(8,128)}), (f32[4096,128]{0,1:T(8,128)}, f32[4096,128]{0,1:T(8,128)})) %all-reduce.12.cloned.1.call-update) | async-done | bytes 4194320 | tf_op jit(solution)/shard_map/psum | solution.py:92
  325.5 7.0 fusion.133
  332.5 1.3 copy.129
  333.8 1.6 broadcast.131.clone.2
  335.4 12.0 %while.47 = (s32[]{:T(128)}, f32[32,128,128]{2,0,1:T(8,128)}, s32[]{:T(128)}, s32[64]{0:T(128)S(1)}, s32[64,128,128]{2,1,0:T(8,128)}, /*index=5*/bf16[32,128,128...) while((s32[]{:T(128)}, f32[32,128,128]{2,0,1:T(8,128)}, ...), condition=%wide.region_11.13_spmd.clone, body=%wide.region_10.12_spmd.clone.sunk | while | flops 472910112 | bytes 15735391 | solution.py:79
  335.5 2.0 gather_fusion.1
  337.5 4.1 fusion.195
  341.6 5.9 fusion.196
  347.5 3.4 copy.119
  350.9 4.5 copy.164
  355.9 102.4 %all-reduce.6.cloned.1.call-done = f32[4096,128]{0,1:T(8,128)} async-done(((f32[4096,128]{0,1:T(8,128)}), f32[4096,128]{0,1:T(8,128)}) %all-reduce.6.cloned.1.call-update) | async-done | bytes 2097168 | tf_op jit(solution)/shard_map/psum | solution.py:101
  458.3 5.5 multiply_reduce_fusion.3
  464.2 1.9 fusion.132
  466.2 1.3 copy.130
  467.5 1.6 broadcast.131.clone.3
  469.1 12.1 %while.48 = (s32[]{:T(128)}, f32[32,128,128]{2,0,1:T(8,128)}, s32[]{:T(128)}, s32[64]{0:T(128)S(1)}, s32[64,128,128]{2,1,0:T(8,128)}, /*index=5*/bf16[32,128,128...) while((s32[]{:T(128)}, f32[32,128,128]{2,0,1:T(8,128)}, ...), condition=%wide.region_16.18_spmd.clone, body=%wide.region_15.17_spmd.clone.sunk | while | flops 472910112 | bytes 15735391 | solution.py:79
  469.2 2.0 gather_fusion.2
  471.2 4.1 fusion.202
  475.3 5.9 fusion.203
  481.2 3.4 copy.122
  484.7 4.6 copy.163
  489.5 102.5 %all-reduce.8.cloned.1.call-done = f32[4096,128]{0,1:T(8,128)} async-done(((f32[4096,128]{0,1:T(8,128)}), f32[4096,128]{0,1:T(8,128)}) %all-reduce.8.cloned.1.call-update) | async-done | bytes 2097168 | tf_op jit(solution)/shard_map/psum | solution.py:101
  592.0 5.3 multiply_reduce_fusion.1
  597.7 1.2 copy-done.6
  599.0 1.8 fusion.131
  600.8 1.3 copy.131
  602.1 1.6 broadcast.131
  603.7 12.3 %while.49 = (s32[]{:T(128)}, f32[32,128,128]{2,0,1:T(8,128)}, s32[]{:T(128)}, s32[64]{0:T(128)S(1)}, s32[64,128,128]{2,1,0:T(8,128)}, /*index=5*/bf16[32,128,128...) while((s32[]{:T(128)}, f32[32,128,128]{2,0,1:T(8,128)}, ...), condition=%wide.region_21.23_spmd.clone, body=%wide.region_20.22_spmd.clone.sunk | while | flops 472910112 | bytes 15735391 | solution.py:79
  603.8 2.0 gather_fusion.3
  605.8 4.1 fusion.209
  609.9 5.9 fusion.210
  616.0 2.7 copy.124
  618.7 3.0 copy.162
  621.9 102.5 %all-reduce.10.cloned.1.call-done = f32[4096,128]{0,1:T(8,128)} async-done(((f32[4096,128]{0,1:T(8,128)}), f32[4096,128]{0,1:T(8,128)}) %all-reduce.10.cloned.1.call-update) | async-done | bytes 2097168 | tf_op jit(solution)/shard_map/psum | solution.py:101
  724.4 5.2 fusion.123
  729.7 1.1 fusion.124
  730.9 0.8 copy.125
  (65 shorter events, 4.0 us)
Async XLA Ops:
  6.5 21.5 %copy-start = (bf16[4096,128]{1,0:T(8,128)(2,1)S(1)}, bf16[4096,128]{1,0:T(8,128)(2,1)}, u32[]{:S(2)}) copy-start(bf16[4096,128]{1,0:T(8,128)(2,1)} %param.16) | copy-start | bytes 3145732
  6.5 54.0 %all-gather.4.cloned.1.call-start = ((), (), s32[]{:S(2)}) async-start(), calls=%async_computation.2 | async-start | bytes 2228224 | tf_op jit(solution)/shard_map/all_gather | solution.py:88
  8.3 3.5 copy-start.8
  16.8 20.7 %all-to-all-start = ((s32[128,1,2]{2,1,0:T(1,128)}), s32[128,1,2]{2,1,0:T(1,128)S(1)}, u32[]{:S(2)}, u32[]{:S(2)}) async-start(s32[128,1,2]{2,1,0:T(1,128)} %copy.108), calls=%async_computation | async-start | bytes 131072 | tf_op jit(solution)/shard_map/all_to_all | solution.py:22
  28.0 174.7 %all-gather.6.cloned.1.call-start = ((), (), s32[]{:S(2)}) async-start(), calls=%async_computation.6 | async-start | bytes 8454144 | tf_op jit(solution)/shard_map/all_gather | solution.py:42
  53.9 106.3 %all-to-all-start.1 = ((bf16[128,2,128,128]{3,2,1,0:T(8,128)(2,1)}), bf16[128,2,128,128]{3,2,1,0:T(8,128)(2,1)}, u32[]{:S(2)}, u32[]{:S(2)}) async-start(bf16[128,2,128,128]{3,2,1,0:T(8,128)(2,1)} %select_select_fusion), calls=%async_computation.1 | async-start | bytes 16777216 | tf_op jit(solution)/shard_map/all_to_all | solution.py:26
  59.9 265.6 %all-reduce.12.cloned.1.call-start = ((), (), s32[]{:S(2)}) async-start(), calls=%async_computation.7 | async-start | bytes 8388608 | tf_op jit(solution)/shard_map/psum | solution.py:92
  164.6 3.2 copy-start.7
  174.2 6.1 copy-start.2
  202.4 255.9 %all-reduce.6.cloned.1.call-start = ((), (), s32[]{:S(2)}) async-start(), calls=%async_computation.3 | async-start | bytes 4194304 | tf_op jit(solution)/shard_map/psum | solution.py:101
  355.4 236.5 %all-reduce.8.cloned.1.call-start = ((), (), s32[]{:S(2)}) async-start(), calls=%async_computation.4 | async-start | bytes 4194304 | tf_op jit(solution)/shard_map/psum | solution.py:101
  458.3 5.5 copy-start.3
  464.2 2.0 copy-start.4
  489.3 235.1 %all-reduce.10.cloned.1.call-start = ((), (), s32[]{:S(2)}) async-start(), calls=%async_computation.5 | async-start | bytes 4194304 | tf_op jit(solution)/shard_map/psum | solution.py:101
  592.0 5.4 copy-start.5
  597.4 1.6 copy-start.6
  724.4 7.2 copy-start.1
Sparse Core Ops, SparseCore 0:
  9.4 49.4 all-gather.3
  62.1 130.2 all-gather.5
  202.5 122.9 all-reduce.11
  355.5 102.6 all-reduce.5
  489.4 102.5 all-reduce.7
  621.8 102.5 all-reduce.9
